TPU v7x, 32 devices: a whole 2x2x4 slice. The times are simulated.
32 devices in a mesh: groups: 2 (over y), seq: 8 (over z, x), head: 2 (over core).
Axes of the slice: x: 2, y: 2, z: 4, core: 2. Of those that a mesh axis runs over, the one named last changes fastest.
Arguments:
- big_queries: bfloat16 [512, 4096], P(('groups', 'seq'), 'head'), parts along dimension 0, may hold values from -160 to 160
- big_keys: bfloat16 [512, 4096], P(('groups', 'seq'), 'head'), parts along dimension 0, may hold values from -8 to 8
- big_values: bfloat16 [512, 4096], P(('groups', 'seq'), 'head'), parts along dimension 0, may hold values from -6 to 6
- small_queries: bfloat16 [512, 1024], P(('groups', 'seq', 'head')), parts along dimension 0, may hold values from -160 to 160
- small_keys: bfloat16 [512, 1024], P(('groups', 'seq', 'head')), parts along dimension 0, may hold values from -8 to 8
- small_values: bfloat16 [512, 1024], P(('groups', 'seq', 'head')), parts along dimension 0, may hold values from -6 to 6
- big_readout: bfloat16 [4096, 64], P('head'), may hold values from -0.75 to 0.75
- small_readout: bfloat16 [1024, 64], replicated, may hold values from -1.5 to 1.5
- guidance: float32 [2], P('groups'), parts along dimension 0, may hold values from 1 to 4
Outputs:
- guided: float32 [256, 128], P(('groups', 'seq')), parts along dimension 0
There are 2 independent parts, one for each index of `groups`. A program takes and returns all parts, laid end to end along the dimension named above; an argument that names none is the same for every part. Nothing has to cross between parts.
All inputs are finite; a program needn't handle non-finite values.
Results may differ from a plain program's by a relative error of at most 0.0035.
Values may be sent and summed in bfloat16 or wider, within the bound.
A program may use at most 64 MiB of HBM per device.

v0:
```python
import math

import jax
import jax.numpy as jnp
from jax import lax
from jax.sharding import PartitionSpec as P

DH = 128


def split_heads(matrix, blocks, parts):
    rows_here, columns = matrix.shape
    shaped = matrix.reshape(blocks, rows_here // blocks, parts, columns // parts)
    shaped = jnp.transpose(shaped, (0, 2, 1, 3))
    return shaped.reshape(blocks * parts, rows_here // blocks, columns // parts)


def copy_heads(matrix, blocks, parts):
    rows_here, columns = matrix.shape
    shaped = jnp.transpose(matrix.reshape(rows_here, parts, columns // parts), (1, 0, 2))
    shaped = jnp.broadcast_to(shaped[None], (blocks, parts, rows_here, columns // parts))
    return shaped.reshape(blocks * parts, rows_here, columns // parts)


def join_heads(stacked, blocks, parts):
    pieces, rows_here, columns = stacked.shape
    shaped = stacked.reshape(blocks, parts, rows_here, columns)
    shaped = jnp.transpose(shaped, (0, 2, 1, 3))
    return shaped.reshape(blocks * rows_here, parts * columns)


def attend(query_rows, key_rows, value_rows):
    query_count = query_rows.shape[0]
    heads_here = query_rows.shape[1] // DH
    key_count = key_rows.shape[0]
    block_height = math.gcd(query_count, 256)
    block_count = query_count // block_height
    query_blocks = query_rows.reshape(block_count, block_height, heads_here, DH)
    key_split = key_rows.reshape(key_count, heads_here, DH)
    value_split = value_rows.reshape(key_count, heads_here, DH)
    score_scale = 1.0 / math.sqrt(DH)

    def one_block(query_block):
        scores = (
            jnp.einsum("qgd,kgd->gqk", query_block, key_split, preferred_element_type=jnp.float32)
            * score_scale
        )
        row_max = jnp.max(scores, axis=2, keepdims=True)
        probs = jnp.exp(scores - row_max)
        totals = jnp.sum(probs, axis=2, keepdims=True)
        weights = probs.astype(jnp.bfloat16)
        accumulated = jnp.einsum(
            "gqk,kgd->gqd", weights, value_split, preferred_element_type=jnp.float32
        )
        attended = accumulated / totals
        attended = jnp.transpose(attended, (1, 0, 2)).reshape(block_height, heads_here * DH)
        return attended.astype(jnp.bfloat16)

    outputs = lax.map(one_block, query_blocks)
    return outputs.reshape(query_count, heads_here * DH)


def shards(
    big_queries,
    big_keys,
    big_values,
    small_queries,
    small_keys,
    small_values,
    big_readout,
    small_readout,
    guidance,
):
    seq_count = lax.axis_size("seq")
    big_heads = big_queries.shape[1] // DH
    big_group = max(big_heads // seq_count, 1)
    big_blocks = max(seq_count // big_heads, 1)
    big_parts = big_heads // big_group
    query_rows = lax.all_to_all(
        split_heads(big_queries, big_blocks, big_parts),
        "seq",
        split_axis=0,
        concat_axis=1,
        tiled=True,
    )[0]
    key_copies, value_copies = (
        lax.all_to_all(
            copy_heads(big_keys, big_blocks, big_parts),
            "seq",
            split_axis=0,
            concat_axis=1,
            tiled=True,
        ),
        lax.all_to_all(
            copy_heads(big_values, big_blocks, big_parts),
            "seq",
            split_axis=0,
            concat_axis=1,
            tiled=True,
        ),
    )
    key_rows = key_copies[0]
    value_rows = value_copies[0]
    big_out = attend(query_rows, key_rows, value_rows)
    big_back = lax.all_to_all(big_out[None], "seq", split_axis=1, concat_axis=0, tiled=True)
    big_attention = join_heads(big_back, big_blocks, big_parts)
    big_partial = jnp.dot(big_attention, big_readout, preferred_element_type=jnp.float32)
    small_heads = small_queries.shape[1] // DH
    small_group = max(small_heads // seq_count, 1)
    small_blocks = max(seq_count // small_heads, 1)
    small_parts = small_heads // small_group
    small_query_rows = lax.all_to_all(
        split_heads(small_queries, small_blocks, small_parts),
        "seq",
        split_axis=0,
        concat_axis=1,
        tiled=True,
    )[0]
    key_copies, value_copies = (
        lax.all_to_all(
            copy_heads(small_keys, small_blocks, small_parts),
            "seq",
            split_axis=0,
            concat_axis=1,
            tiled=True,
        ),
        lax.all_to_all(
            copy_heads(small_values, small_blocks, small_parts),
            "seq",
            split_axis=0,
            concat_axis=1,
            tiled=True,
        ),
    )
    small_key_rows, small_value_rows = (
        lax.all_gather(key_copies[0], "head", axis=0, tiled=True),
        lax.all_gather(value_copies[0], "head", axis=0, tiled=True),
    )
    small_out = attend(small_query_rows, small_key_rows, small_value_rows)
    small_back = lax.all_to_all(small_out[None], "seq", split_axis=1, concat_axis=0, tiled=True)
    small_attention = join_heads(small_back, small_blocks, small_parts)
    small_latent = jnp.dot(small_attention, small_readout, preferred_element_type=jnp.float32)
    weight_value = guidance[0]
    core_index = lax.axis_index("head")
    placed = lax.dynamic_update_slice(
        jnp.zeros_like(big_partial),
        small_latent,
        (core_index * small_latent.shape[0], jnp.zeros((), jnp.int32)),
    )
    blended = lax.psum((1.0 + weight_value) * big_partial - weight_value * placed, "head")
    return blended.reshape(blended.shape[0] // 2, 2 * blended.shape[1])


def solution(mesh):
    placed = (
        P(("groups", "seq"), "head"),
        P(("groups", "seq"), "head"),
        P(("groups", "seq"), "head"),
        P(("groups", "seq", "head"), None),
        P(("groups", "seq", "head"), None),
        P(("groups", "seq", "head"), None),
        P("head", None),
        P(),
        P("groups"),
    )
    return jax.shard_map(
        shards, mesh=mesh, in_specs=placed, out_specs=P(("groups", "seq"), None), check_vma=False
    )
```

profile of v0, /device:TPU:0, one launch (start us, length us, event | category | flops | bytes accessed | tf_op | source)
XLA Modules:
  0.0 93.8 jit_solution(16511722047531669533)
XLA Ops:
  0.0 0.0 copy-start
  0.0 0.8 copy.72
  0.8 0.6 copy.60
  1.4 0.0 copy-start.5
  1.4 7.4 %all-to-all-start.6 = ((bf16[8,16,128]{2,1,0:T(8,128)(2,1)}), bf16[8,16,128]{2,1,0:T(8,128)(2,1)S(1)}, u32[]{:S(2)}, u32[]{:S(2)}) async-start(bf16[8,16,128]{2,1,0:T(8,128)(2,1)} %copy.60), calls=%async_computation.6 | async-start | bytes 65536 | tf_op jit(solution)/shard_map/all_to_all | solution.py:127
  8.8 0.0 copy-done.5
  8.9 0.0 copy-start.6
  8.9 0.7 copy-done.6
  9.6 0.6 copy.59
  10.2 0.0 copy-start.1
  10.2 5.3 %all-to-all-done.6 = bf16[8,16,128]{2,1,0:T(8,128)(2,1)S(1)} async-done(((bf16[8,16,128]{2,1,0:T(8,128)(2,1)}), bf16[8,16,128]{2,1,0:T(8,128)(2,1)S(1)}, u32[]{:S(2)}, u32[]{:S(2)}) %all-to-all-start.6) | async-done | bytes 32800 | tf_op jit(solution)/shard_map/all_to_all | solution.py:127
  15.5 3.3 %all-to-all-start.5 = ((bf16[8,16,128]{2,1,0:T(8,128)(2,1)}), bf16[8,16,128]{2,1,0:T(8,128)(2,1)S(1)}, u32[]{:S(2)}, u32[]{:S(2)}) async-start(bf16[8,16,128]{2,1,0:T(8,128)(2,1)} %copy.59), calls=%async_computation.5 | async-start | bytes 65536 | tf_op jit(solution)/shard_map/all_to_all | solution.py:120
  18.9 0.6 copy.58
  19.5 6.0 %all-to-all-done.5 = bf16[8,16,128]{2,1,0:T(8,128)(2,1)S(1)} async-done(((bf16[8,16,128]{2,1,0:T(8,128)(2,1)}), bf16[8,16,128]{2,1,0:T(8,128)(2,1)S(1)}, u32[]{:S(2)}, u32[]{:S(2)}) %all-to-all-start.5) | async-done | bytes 32800 | tf_op jit(solution)/shard_map/all_to_all | solution.py:120
  25.5 3.3 %all-to-all-start.4 = ((bf16[8,16,128]{2,1,0:T(8,128)(2,1)}), bf16[8,16,128]{2,1,0:T(8,128)(2,1)S(1)}, u32[]{:S(2)}, u32[]{:S(2)}) async-start(bf16[8,16,128]{2,1,0:T(8,128)(2,1)} %copy.58), calls=%async_computation.4 | async-start | bytes 65536 | tf_op jit(solution)/shard_map/all_to_all | solution.py:112
  28.8 0.0 copy-done.1
  28.8 0.0 copy-start.2
  28.9 0.7 copy.93
  29.5 0.3 copy-done.2
  29.8 0.0 copy-start.3
  29.8 0.7 copy.95
  30.5 0.2 copy-done.3
  30.8 0.7 copy.94
  31.4 1.8 %all_gather.7 = bf16[256,128]{1,0:T(8,128)(2,1)S(1)} all-gather(bf16[128,128]{1,0:T(8,128)(2,1)S(1)} %bitcast.91), channel_id=1, replica_groups=mesh['groups'=2,'seq'=8,'head'=2] {'head'}, dimensions={0}, use_global_device_ids=true | all-gather | bytes 98304 | tf_op jit(solution)/shard_map/all_gather | solution.py:137
  33.3 1.8 %all_gather.6 = bf16[256,128]{1,0:T(8,128)(2,1)S(1)} all-gather(bf16[128,128]{1,0:T(8,128)(2,1)S(1)} %bitcast.92), channel_id=1, replica_groups=mesh['groups'=2,'seq'=8,'head'=2] {'head'}, dimensions={0}, use_global_device_ids=true | all-gather | bytes 98304 | tf_op jit(solution)/shard_map/all_gather | solution.py:136
  35.1 0.4 all-to-all-done.4
  35.5 5.6 %all-to-all-start.1 = ((bf16[8,32,256]{2,1,0:T(8,128)(2,1)}), bf16[8,32,256]{2,1,0:T(8,128)(2,1)S(1)}, u32[]{:S(2)}, u32[]{:S(2)}) async-start(bf16[8,32,256]{2,1,0:T(8,128)(2,1)} %bitcast.75), calls=%async_computation.1 | async-start | bytes 262144 | tf_op jit(solution)/shard_map/all_to_all | solution.py:87
  41.0 0.2 fusion.19
  41.3 7.1 %all-to-all-done.1 = bf16[8,32,256]{2,1,0:T(8,128)(2,1)S(1)} async-done(((bf16[8,32,256]{2,1,0:T(8,128)(2,1)}), bf16[8,32,256]{2,1,0:T(8,128)(2,1)S(1)}, u32[]{:S(2)}, u32[]{:S(2)}) %all-to-all-start.1) | async-done | bytes 131104 | tf_op jit(solution)/shard_map/all_to_all | solution.py:87
  48.4 3.4 %all-to-all-start = ((bf16[8,32,256]{2,1,0:T(8,128)(2,1)}), bf16[8,32,256]{2,1,0:T(8,128)(2,1)S(1)}, u32[]{:S(2)}, u32[]{:S(2)}) async-start(bf16[8,32,256]{2,1,0:T(8,128)(2,1)} %bitcast.78), calls=%async_computation | async-start | bytes 262144 | tf_op jit(solution)/shard_map/all_to_all | solution.py:79
  51.8 0.2 fusion.12
  51.9 0.2 fusion.3
  52.2 0.1 copy.96
  52.2 0.5 broadcast.21
  52.7 0.8 reduce.5
  53.6 0.6 reshape.126
  54.2 4.8 %all-to-all-done = bf16[8,32,256]{2,1,0:T(8,128)(2,1)S(1)} async-done(((bf16[8,32,256]{2,1,0:T(8,128)(2,1)}), bf16[8,32,256]{2,1,0:T(8,128)(2,1)S(1)}, u32[]{:S(2)}, u32[]{:S(2)}) %all-to-all-start) | async-done | bytes 131104 | tf_op jit(solution)/shard_map/all_to_all | solution.py:79
  59.0 3.4 %all-to-all-start.2 = ((bf16[8,32,256]{2,1,0:T(8,128)(2,1)}), bf16[8,32,256]{2,1,0:T(8,128)(2,1)S(1)}, u32[]{:S(2)}, u32[]{:S(2)}) async-start(bf16[8,32,256]{2,1,0:T(8,128)(2,1)} %bitcast.77), calls=%async_computation.2 | async-start | bytes 262144 | tf_op jit(solution)/shard_map/all_to_all | solution.py:94
  62.4 0.2 fusion.18
  62.7 0.1 fusion.5
  62.8 6.9 %all-to-all-done.2 = bf16[8,32,256]{2,1,0:T(8,128)(2,1)S(1)} async-done(((bf16[8,32,256]{2,1,0:T(8,128)(2,1)}), bf16[8,32,256]{2,1,0:T(8,128)(2,1)S(1)}, u32[]{:S(2)}, u32[]{:S(2)}) %all-to-all-start.2) | async-done | bytes 131104 | tf_op jit(solution)/shard_map/all_to_all | solution.py:94
  69.7 3.3 %all-to-all-start.7 = ((bf16[8,2,1024]{2,1,0:T(2,128)(2,1)}), bf16[8,2,1024]{2,1,0:T(2,128)(2,1)S(1)}, u32[]{:S(2)}, u32[]{:S(2)}) async-start(bf16[8,2,1024]{2,1,0:T(2,128)(2,1)} %reshape.126), calls=%async_computation.7 | async-start | bytes 65536 | tf_op jit(solution)/shard_map/all_to_all | solution.py:140
  73.1 0.2 fusion.1
  73.3 0.2 copy.56
  73.5 1.4 %reduce.4 = bf16[256,256]{1,0:T(8,128)(2,1)S(1)} reduce(bf16[256,1,256]{2,1,0:T(2,128)(2,1)S(1)} %bitcast.83, bf16[]{:T(256)} %broadcast.21), dimensions={1}, to_apply=%bitcast.63.reduce_sub_computation | reduce | bytes 262146
  74.9 0.7 reshape.124
  75.6 4.0 %all-to-all-done.7 = bf16[8,2,1024]{2,1,0:T(2,128)(2,1)S(1)} async-done(((bf16[8,2,1024]{2,1,0:T(2,128)(2,1)}), bf16[8,2,1024]{2,1,0:T(2,128)(2,1)S(1)}, u32[]{:S(2)}, u32[]{:S(2)}) %all-to-all-start.7) | async-done | bytes 32800 | tf_op jit(solution)/shard_map/all_to_all | solution.py:140
  79.7 3.4 %all-to-all-start.3 = ((bf16[8,2,4096]{2,1,0:T(2,128)(2,1)}), bf16[8,2,4096]{2,1,0:T(2,128)(2,1)S(1)}, u32[]{:S(2)}, u32[]{:S(2)}) async-start(bf16[8,2,4096]{2,1,0:T(2,128)(2,1)} %reshape.124), calls=%async_computation.3 | async-start | bytes 262144 | tf_op jit(solution)/shard_map/all_to_all | solution.py:105
  83.7 0.0 copy-start.4
  83.8 0.8 copy-done.4
  84.6 0.1 convolution_dynamic-update-slice_fusion
  84.7 5.6 %all-to-all-done.3 = bf16[8,2,4096]{2,1,0:T(2,128)(2,1)S(1)} async-done(((bf16[8,2,4096]{2,1,0:T(2,128)(2,1)}), bf16[8,2,4096]{2,1,0:T(2,128)(2,1)S(1)}, u32[]{:S(2)}, u32[]{:S(2)}) %all-to-all-start.3) | async-done | bytes 131104 | tf_op jit(solution)/shard_map/all_to_all | solution.py:105
  90.3 0.1 reshape.125
  90.5 0.0 copy-done
  90.5 0.2 fusion.4
  90.7 0.1 reshape.123
  90.8 3.1 %psum.7 = f32[16,128]{1,0:T(8,128)} all-reduce(f32[16,128]{1,0:T(8,128)S(1)} %reshape.123), channel_id=1, replica_groups=mesh['groups'=2,'seq'=8,'head'=2] {'head'}, use_global_device_ids=true, to_apply=%region_4.5 | all-reduce | flops 2048 | bytes 16384 | tf_op jit(solution)/shard_map/psum | solution.py:150
  (13 shorter events, 0.2 us)
Async XLA Ops:
  0.0 90.5 %copy-start = (bf16[2048,64]{0,1:T(8,128)(2,1)S(1)}, bf16[2048,64]{0,1:T(8,128)(2,1)}, u32[]{:S(2)}) copy-start(bf16[2048,64]{0,1:T(8,128)(2,1)} %param.15) | copy-start | bytes 786436
  1.4 7.4 %copy-start.5 = (bf16[16,1024]{1,0:T(8,128)(2,1)S(1)}, bf16[16,1024]{1,0:T(8,128)(2,1)}, u32[]{:S(2)}) copy-start(bf16[16,1024]{1,0:T(8,128)(2,1)} %param.12) | copy-start | bytes 98308
  1.4 14.1 %all-to-all-start.6 = ((bf16[8,16,128]{2,1,0:T(8,128)(2,1)}), bf16[8,16,128]{2,1,0:T(8,128)(2,1)S(1)}, u32[]{:S(2)}, u32[]{:S(2)}) async-start(bf16[8,16,128]{2,1,0:T(8,128)(2,1)} %copy.60), calls=%async_computation.6 | async-start | bytes 65536 | tf_op jit(solution)/shard_map/all_to_all | solution.py:127
  8.9 0.8 copy-start.6
  10.2 18.6 %copy-start.1 = (bf16[32,2048]{1,0:T(8,128)(2,1)S(1)}, bf16[32,2048]{1,0:T(8,128)(2,1)}, u32[]{:S(2)}) copy-start(bf16[32,2048]{1,0:T(8,128)(2,1)} %param.10) | copy-start | bytes 393220
  15.5 10.0 %all-to-all-start.5 = ((bf16[8,16,128]{2,1,0:T(8,128)(2,1)}), bf16[8,16,128]{2,1,0:T(8,128)(2,1)S(1)}, u32[]{:S(2)}, u32[]{:S(2)}) async-start(bf16[8,16,128]{2,1,0:T(8,128)(2,1)} %copy.59), calls=%async_computation.5 | async-start | bytes 65536 | tf_op jit(solution)/shard_map/all_to_all | solution.py:120
  25.5 10.0 %all-to-all-start.4 = ((bf16[8,16,128]{2,1,0:T(8,128)(2,1)}), bf16[8,16,128]{2,1,0:T(8,128)(2,1)S(1)}, u32[]{:S(2)}, u32[]{:S(2)}) async-start(bf16[8,16,128]{2,1,0:T(8,128)(2,1)} %copy.58), calls=%async_computation.4 | async-start | bytes 65536 | tf_op jit(solution)/shard_map/all_to_all | solution.py:112
  28.8 1.0 %copy-start.2 = (bf16[32,2048]{1,0:T(8,128)(2,1)S(1)}, bf16[32,2048]{1,0:T(8,128)(2,1)}, u32[]{:S(2)}) copy-start(bf16[32,2048]{1,0:T(8,128)(2,1)} %param.9) | copy-start | bytes 393220
  29.8 0.9 copy-start.3
  35.5 12.9 %all-to-all-start.1 = ((bf16[8,32,256]{2,1,0:T(8,128)(2,1)}), bf16[8,32,256]{2,1,0:T(8,128)(2,1)S(1)}, u32[]{:S(2)}, u32[]{:S(2)}) async-start(bf16[8,32,256]{2,1,0:T(8,128)(2,1)} %bitcast.75), calls=%async_computation.1 | async-start | bytes 262144 | tf_op jit(solution)/shard_map/all_to_all | solution.py:87
  48.4 10.7 %all-to-all-start = ((bf16[8,32,256]{2,1,0:T(8,128)(2,1)}), bf16[8,32,256]{2,1,0:T(8,128)(2,1)S(1)}, u32[]{:S(2)}, u32[]{:S(2)}) async-start(bf16[8,32,256]{2,1,0:T(8,128)(2,1)} %bitcast.78), calls=%async_computation | async-start | bytes 262144 | tf_op jit(solution)/shard_map/all_to_all | solution.py:79
  59.0 10.7 %all-to-all-start.2 = ((bf16[8,32,256]{2,1,0:T(8,128)(2,1)}), bf16[8,32,256]{2,1,0:T(8,128)(2,1)S(1)}, u32[]{:S(2)}, u32[]{:S(2)}) async-start(bf16[8,32,256]{2,1,0:T(8,128)(2,1)} %bitcast.77), calls=%async_computation.2 | async-start | bytes 262144 | tf_op jit(solution)/shard_map/all_to_all | solution.py:94
  69.7 10.0 %all-to-all-start.7 = ((bf16[8,2,1024]{2,1,0:T(2,128)(2,1)}), bf16[8,2,1024]{2,1,0:T(2,128)(2,1)S(1)}, u32[]{:S(2)}, u32[]{:S(2)}) async-start(bf16[8,2,1024]{2,1,0:T(2,128)(2,1)} %reshape.126), calls=%async_computation.7 | async-start | bytes 65536 | tf_op jit(solution)/shard_map/all_to_all | solution.py:140
  79.7 10.7 %all-to-all-start.3 = ((bf16[8,2,4096]{2,1,0:T(2,128)(2,1)}), bf16[8,2,4096]{2,1,0:T(2,128)(2,1)S(1)}, u32[]{:S(2)}, u32[]{:S(2)}) async-start(bf16[8,2,4096]{2,1,0:T(2,128)(2,1)} %reshape.124), calls=%async_computation.3 | async-start | bytes 262144 | tf_op jit(solution)/shard_map/all_to_all | solution.py:105
  83.7 0.9 copy-start.4
where the time goes:
time: 94.8 us; the launch traced here: 93.8 us
  waiting for transfers between devices  40.1 us (42%)
  starting transfers between devices  33.1 us (35%)
  local copies, waits for them, and re-layouts  9.24 us (10%)
  blocking collectives  6.74 us (7%)
  other arithmetic  2.51 us (3%)
  matrix products  1.29 us (1%)
    all_to_all x1, starting transfers between devices, shards(): lax.all_to_all(copy_heads(small_values, small_blocks, small_parts), 'seq'...  7.41 us
    all_to_all x1, waiting for transfers between devices, shards(): lax.all_to_all(copy_heads(big_keys, big_blocks, big_parts), 'seq', split_...  7.09 us
    all_to_all x1, waiting for transfers between devices, shards(): lax.all_to_all(copy_heads(big_values, big_blocks, big_parts), 'seq', spli...  6.9 us
    all_to_all x1, waiting for transfers between devices, shards(): lax.all_to_all(copy_heads(small_keys, small_blocks, small_parts), 'seq',...  6 us
    all_to_all x1, waiting for transfers between devices, shards(): lax.all_to_all(big_out[None], 'seq', split_axis=1, concat_axis=0, tiled=T...  5.59 us
    all_to_all x1, starting transfers between devices, shards(): lax.all_to_all(copy_heads(big_keys, big_blocks, big_parts), 'seq', split_...  5.57 us
    all_to_all x1, waiting for transfers between devices, shards(): lax.all_to_all(copy_heads(small_values, small_blocks, small_parts), 'seq'...  5.29 us
    unnamed x26, local copies, waits for them, and re-layouts  4.96 us
  transfers between devices with their start and end apart: 8, of which 8 were waited for; matrix products, arithmetic and copies ran while one was open for 10% of the time, Pallas kernels for 0%

commit v1 on v0

--- a/solution.py
+++ b/solution.py
@@ -1,8 +1,11 @@
+import functools
 import math
 
 import jax
 import jax.numpy as jnp
 from jax import lax
+from jax.experimental import pallas as pl
+from jax.experimental.pallas import tpu as pltpu
 from jax.sharding import PartitionSpec as P
 
 DH = 128
@@ -60,7 +63,7 @@
     return outputs.reshape(query_count, heads_here * DH)
 
 
-def shards(
+def exchanged(
     big_queries,
     big_keys,
     big_values,
@@ -151,6 +154,349 @@
     return blended.reshape(blended.shape[0] // 2, 2 * blended.shape[1])
 
 
+MESH = pl.DeviceIdType.MESH
+
+
+def far_first(count):
+    return sorted(range(1, count), key=lambda offset: -min(offset, count - offset))
+
+
+def softmax_parts(query_head, key_head):
+    scores = lax.dot_general(
+        query_head, key_head, (((1,), (1,)), ((), ())), preferred_element_type=jnp.float32
+    ) * (1.0 / math.sqrt(DH))
+    row_max = jnp.max(scores, axis=1, keepdims=True)
+    probs = jnp.exp(scores - row_max)
+    totals = jnp.sum(probs, axis=1, keepdims=True)
+    return probs.astype(jnp.bfloat16), totals
+
+
+def weigh(weights, totals, value_head):
+    accumulated = jnp.dot(weights, value_head, preferred_element_type=jnp.float32)
+    return (accumulated / totals).astype(jnp.bfloat16)
+
+
+def fused_kernel(
+    n,
+    m,
+    guidance,
+    big_q,
+    big_k,
+    big_v,
+    small_q,
+    small_k,
+    small_v,
+    big_read,
+    small_read,
+    out,
+    all_q,
+    all_k,
+    all_v,
+    few_q,
+    few_k,
+    few_v,
+    read_big,
+    read_small,
+    weights,
+    latent,
+    small_part,
+    stage,
+    arrived,
+    own_sem,
+    big_send,
+    big_recv,
+    small_send,
+    small_recv,
+    back_send,
+    back_recv,
+):
+    group = lax.axis_index("groups")
+    me = lax.axis_index("seq")
+    core = lax.axis_index("head")
+    rows = big_q.shape[0]
+    width = all_q.shape[1]
+    few_rows = small_q.shape[0]
+    few_width = few_q.shape[1]
+    heads_here = width // DH
+    few_heads = few_width // DH
+    lat = big_read.shape[1]
+    half = stage.shape[1]
+    order = far_first(n)
+
+    def ahead(offset):
+        return lax.rem(me + offset, n)
+
+    def behind(offset):
+        return lax.rem(me + n - offset, n)
+
+    def window(ref, index, size):
+        return ref.at[:, pl.ds(pl.multiple_of(index * size, size), size)]
+
+    def big_land(ref, seq):
+        return ref.at[pl.ds(pl.multiple_of(seq * rows, rows), rows), :]
+
+    def few_land(ref, seq, which):
+        start = pl.multiple_of((seq * m + which) * few_rows, few_rows)
+        return ref.at[pl.ds(start, few_rows), :]
+
+    big_pairs = ((big_k, all_k), (big_q, all_q), (big_v, all_v))
+    few_pairs = ((small_k, few_k), (small_q, few_q), (small_v, few_v))
+
+    def big_copy(item, offset, landing):
+        source, target = big_pairs[item]
+        peer = ahead(offset)
+        return pltpu.make_async_remote_copy(
+            src_ref=window(source, peer, width),
+            dst_ref=big_land(target, landing),
+            send_sem=big_send.at[item, offset],
+            recv_sem=big_recv.at[item, offset],
+            device_id=(group, peer, core),
+            device_id_type=MESH,
+        )
+
+    def few_copy(item, offset, landing, which):
+        source, target = few_pairs[item]
+        peer = ahead(offset)
+        return pltpu.make_async_remote_copy(
+            src_ref=window(source, peer, few_width),
+            dst_ref=few_land(target, landing, which),
+            send_sem=small_send.at[item, offset],
+            recv_sem=small_recv.at[item, offset, which],
+            device_id=(group, peer, 0),
+            device_id_type=MESH,
+        )
+
+    def back_copy(offset, turn, slot_core):
+        peer = ahead(offset)
+        return pltpu.make_async_remote_copy(
+            src_ref=stage.at[peer],
+            dst_ref=arrived.at[offset, slot_core],
+            send_sem=back_send.at[offset, turn],
+            recv_sem=back_recv.at[offset, slot_core],
+            device_id=(group, peer, lax.rem(core + turn, m)),
+            device_id_type=MESH,
+        )
+
+    barrier = pltpu.get_barrier_semaphore()
+    for offset in range(n):
+        for turn in range(m):
+            if offset or turn:
+                pl.semaphore_signal(
+                    barrier,
+                    inc=1,
+                    device_id=(group, ahead(offset), lax.rem(core + turn, m)),
+                    device_id_type=MESH,
+                )
+
+    read_rows = pl.ds(pl.multiple_of(me * width, width), width)
+    few_read_rows = pl.ds(pl.multiple_of(me * few_width, few_width), few_width)
+    own = [
+        pltpu.make_async_copy(
+            window(source, me, width), big_land(target, me), own_sem.at[item]
+        )
+        for item, (source, target) in enumerate(big_pairs)
+    ]
+    own.append(pltpu.make_async_copy(big_read.at[read_rows, :], read_big, own_sem.at[3]))
+    own.append(
+        pltpu.make_async_copy(small_read.at[few_read_rows, :], read_small, own_sem.at[4])
+    )
+    few_own = [
+        pltpu.make_async_copy(
+            window(source, me, few_width), few_land(target, me, 0), own_sem.at[5 + item]
+        )
+        for item, (source, target) in enumerate(few_pairs)
+    ]
+    for copy in own:
+        copy.start()
+
+    @pl.when(core == 0)
+    def _():
+        for copy in few_own:
+            copy.start()
+
+    pl.semaphore_wait(barrier, n * m - 1)
+
+    for offset in order:
+        for item in range(3):
+            few_copy(item, offset, me, core).start()
+
+    @pl.when(core != 0)
+    def _():
+        for item in range(3):
+            few_copy(item, 0, me, core).start()
+
+    for items in ((0, 1), (2,)):
+        for offset in order:
+            for item in items:
+                big_copy(item, offset, me).start()
+
+    for copy in own:
+        copy.wait()
+    weight_value = guidance[0]
+    lanes = lax.broadcasted_iota(jnp.int32, (latent.shape[0] // 2, 2 * lat), 1)
+
+    def paired(attended, readout):
+        doubled = jnp.concatenate([readout, readout], axis=1)
+        latent[...] = jnp.dot(attended, doubled, preferred_element_type=jnp.float32)
+        even = latent[pl.ds(0, latent.shape[0] // 2, stride=2), :]
+        odd = latent[pl.ds(1, latent.shape[0] // 2, stride=2), :]
+        return jnp.where(lanes < lat, even, odd)
+
+    @pl.when(core == 0)
+    def _():
+        for copy in few_own:
+            copy.wait()
+        for which in range(m):
+            for offset in range(n):
+                if offset or which:
+                    for item in range(3):
+                        few_copy(item, offset, behind(offset), which).wait_recv()
+        pieces = []
+        for head in range(few_heads):
+            columns = slice(head * DH, (head + 1) * DH)
+            probs, totals = softmax_parts(few_q[:, columns], few_k[:, columns])
+            pieces.append(weigh(probs, totals, few_v[:, columns]))
+        attended = pieces[0] if few_heads == 1 else jnp.concatenate(pieces, axis=1)
+        small_part[...] = weight_value * paired(attended, read_small[...])
+
+    @pl.when(core != 0)
+    def _():
+        small_part[...] = jnp.zeros_like(small_part)
+
+    for offset in order:
+        for item in (0, 1):
+            big_copy(item, offset, behind(offset)).wait_recv()
+    totals_of = []
+    for head in range(heads_here):
+        columns = slice(head * DH, (head + 1) * DH)
+        probs, totals = softmax_parts(all_q[:, columns], all_k[:, columns])
+        weights[head] = probs
+        totals_of.append(totals)
+    for offset in order:
+        big_copy(2, offset, behind(offset)).wait_recv()
+    pieces = [
+        weigh(weights[head], totals_of[head], all_v[:, head * DH : (head + 1) * DH])
+        for head in range(heads_here)
+    ]
+    attended = pieces[0] if heads_here == 1 else jnp.concatenate(pieces, axis=1)
+    term = (1.0 + weight_value) * paired(attended, read_big[...]) - small_part[...]
+    stage[...] = term.reshape(n, half, 2 * lat)
+    arrived[0, core] = stage[me]
+
+    for offset in order + [0]:
+        for turn in range(m):
+            if offset or turn:
+                back_copy(offset, turn, core).start()
+    for offset in range(n):
+        for slot_core in range(m):
+            if offset:
+                back_copy(offset, 0, slot_core).wait_recv()
+    for turn in range(1, m):
+        back_copy(0, turn, lax.rem(core + turn, m)).wait_recv()
+    out[...] = jnp.sum(arrived[...].reshape(n * m, half, 2 * lat), axis=0)
+
+    for offset in order:
+        for item in range(3):
+            few_copy(item, offset, me, core).wait_send()
+            big_copy(item, offset, me).wait_send()
+
+    @pl.when(core != 0)
+    def _():
+        for item in range(3):
+            few_copy(item, 0, me, core).wait_send()
+
+    for offset in order + [0]:
+        for turn in range(m):
+            if offset or turn:
+                back_copy(offset, turn, core).wait_send()
+
+
+def fused(
+    n,
+    m,
+    big_queries,
+    big_keys,
+    big_values,
+    small_queries,
+    small_keys,
+    small_values,
+    big_readout,
+    small_readout,
+    guidance,
+):
+    rows, columns = big_queries.shape
+    few_rows, few_columns = small_queries.shape
+    width, few_width = columns // n, few_columns // n
+    tokens = rows * n
+    lat = big_readout.shape[1]
+    half = rows // 2
+    kind = jnp.bfloat16
+    dma = pltpu.SemaphoreType.DMA
+    return pl.pallas_call(
+        functools.partial(fused_kernel, n, m),
+        out_shape=jax.ShapeDtypeStruct((half, 2 * lat), jnp.float32),
+        in_specs=[pl.BlockSpec(memory_space=pltpu.SMEM)]
+        + [pl.BlockSpec(memory_space=pl.ANY)] * 8,
+        out_specs=pl.BlockSpec(memory_space=pltpu.VMEM),
+        scratch_shapes=[
+            pltpu.VMEM((tokens, width), kind),
+            pltpu.VMEM((tokens, width), kind),
+            pltpu.VMEM((tokens, width), kind),
+            pltpu.VMEM((tokens, few_width), kind),
+            pltpu.VMEM((tokens, few_width), kind),
+            pltpu.VMEM((tokens, few_width), kind),
+            pltpu.VMEM((width, lat), kind),
+            pltpu.VMEM((few_width, lat), kind),
+            pltpu.VMEM((width // DH, tokens, tokens), kind),
+            pltpu.VMEM((tokens, 2 * lat), jnp.float32),
+            pltpu.VMEM((tokens // 2, 2 * lat), jnp.float32),
+            pltpu.VMEM((n, half, 2 * lat), jnp.float32),
+            pltpu.VMEM((n, m, half, 2 * lat), jnp.float32),
+            dma((8,)),
+            dma((3, n)),
+            dma((3, n)),
+            dma((3, n)),
+            dma((3, n, m)),
+            dma((n, m)),
+            dma((n, m)),
+        ],
+        compiler_params=pltpu.CompilerParams(collective_id=0, has_side_effects=True),
+        name="fused_window",
+    )(
+        guidance,
+        big_queries,
+        big_keys,
+        big_values,
+        small_queries,
+        small_keys,
+        small_values,
+        big_readout,
+        small_readout,
+    )
+
+
+def fits(n, m, big_queries, small_queries, lat):
+    rows, columns = big_queries.shape
+    few_rows, few_columns = small_queries.shape
+    return (
+        n > 1
+        and m > 1
+        and n * rows <= 512
+        and columns % (n * DH) == 0
+        and few_columns % (n * DH) == 0
+        and rows == m * few_rows
+        and few_rows % 16 == 0
+        and 2 * lat == 128
+    )
+
+
+def shards(*arguments):
+    n, m = lax.axis_size("seq"), lax.axis_size("head")
+    if fits(n, m, arguments[0], arguments[3], arguments[6].shape[1]):
+        return fused(n, m, *arguments)
+    return exchanged(*arguments)
+
+
 def solution(mesh):
     placed = (
         P(("groups", "seq"), "head"),

time: 94.8 us -> 31.3 us (0.33)
  waiting for transfers between devices: 40.1 us -> 0 us
  starting transfers between devices: 33.1 us -> 0 us
  Pallas kernels: 0 us -> 26.4 us
  blocking collectives: 6.74 us -> 0 us
  local copies, waits for them, and re-layouts: 9.24 us -> 4.03 us
  other arithmetic: 2.51 us -> 0 us
  matrix products: 1.29 us -> 0 us
    all_to_all x8 -> x0, waiting for transfers between devices: 40.1 us -> none  [the longest x1 7.09 us: shards(): lax.all_to_all(copy_heads(big_keys, big_blocks, big_parts), 'seq', split_...]
    all_to_all x8 -> x0, starting transfers between devices: 33.1 us -> none  [the longest x1 7.41 us: shards(): lax.all_to_all(copy_heads(small_values, small_blocks, small_parts), 'seq'...]
    pallas_call x0 -> x1, Pallas kernels: none -> 26.4 us  [fused(): pl.pallas_call(functools.partial(fused_kernel, n, m), out_shape=jax.Shape...]
    all_gather x2 -> x0, blocking collectives: 3.68 us -> none  [the longest x1 1.84 us: shards(): lax.all_gather(key_copies[0], 'head', axis=0, tiled=True)]
    psum x1 -> x0, blocking collectives: 3.06 us -> none  [shards(): lax.psum((1.0 + weight_value) * big_partial - weight_value * placed, 'head')]
    reshape x6 -> x0, local copies, waits for them, and re-layouts: 2.69 us -> none  [the longest x2 1.32 us: copy_heads(): matrix.reshape(rows_here, parts, columns // parts)]
    unnamed x2 -> x0, other arithmetic: 2.23 us -> none
    dot_general x6 -> x0, matrix products: 1.29 us -> none  [the longest x2 0.49 us: one_block(): jnp.einsum('qgd,kgd->gqk', query_block, key_split, preferred_element_type...]
  transfers between devices with their start and end apart: 8 -> 0, of which waited for: 8 -> 0; matrix products, arithmetic and copies ran while one was open for 10% -> 0% of each run, Pallas kernels for 0% -> 0%
where the time goes in v1:
time: 31.3 us; the launch traced here: 31.1 us
  Pallas kernels  26.4 us (84%)
  local copies, waits for them, and re-layouts  4.03 us (13%)
  between operations  0.71 us (2%)
    pallas_call x1, Pallas kernels, fused(): pl.pallas_call(functools.partial(fused_kernel, n, m), out_shape=jax.Shape...  26.4 us
    unnamed x5, local copies, waits for them, and re-layouts  4.03 us

profile of v1, /device:TPU:0, one launch (start us, length us, event | category | flops | bytes accessed | tf_op | source)
XLA Modules:
  0.0 31.1 jit_solution(18124781211245106337)
XLA Ops:
  0.0 0.0 copy-start
  0.7 1.7 %copy.11.small_read = bf16[1024,64]{1,0:T(8,128)(2,1)} copy(bf16[1024,64]{0,1:T(8,128)(2,1)} %param.16) | data formatting | bytes 262144 | tf_op args[7]
  2.4 0.0 copy-done
  2.4 1.0 %copy.10.big_read = bf16[2048,64]{1,0:T(8,128)(2,1)} copy(bf16[2048,64]{0,1:T(8,128)(2,1)S(1)} %copy-done) | data formatting | bytes 524288 | tf_op args[6]
  3.4 26.4 %fused_window.1 = f32[16,128]{1,0:T(8,128)} custom-call(f32[1]{0:T(128)S(6)} %copy.13.guidance, bf16[32,2048]{1,0:T(8,128)(2,1)} %big_q.1, bf16[32,2048]{1,0:T(8,128)(2,1)} %big_k.1, bf16[32,2048]{1,0:T(8,128)(2,1)} %big_v.1, bf16[16,1024]{1,0:T(8,128)(2,1)} %small_q.1, bf16[16,1024]{1,0:T(8,128)(2,1)} %small_k.1, bf16[16,1024]{1,0:T(8,128)(2,1)} %small_v.1, ...), custom_call_target="tpu_custom_call" | custom-call | tf_op jit(solution)/shard_map/fused_window/pallas_call | solution.py:435
  29.8 1.3 %copy.14 = f32[16,128]{1,0:T(8,128)} copy(f32[16,128]{1,0:T(8,128)} %fused_window.1) | data formatting | bytes 16384
Async XLA Ops:
  0.0 2.4 %copy-start = (bf16[2048,64]{0,1:T(8,128)(2,1)S(1)}, bf16[2048,64]{0,1:T(8,128)(2,1)}, u32[]{:S(2)}) copy-start(bf16[2048,64]{0,1:T(8,128)(2,1)} %param.15) | copy-start | bytes 786436

commit v2 on v1

--- a/solution.py
+++ b/solution.py
@@ -202,6 +202,7 @@
     small_part,
     stage,
     arrived,
+    guide,
     own_sem,
     big_send,
     big_recv,
@@ -219,7 +220,7 @@
     few_width = few_q.shape[1]
     heads_here = width // DH
     few_heads = few_width // DH
-    lat = big_read.shape[1]
+    lat = big_read.shape[0]
     half = stage.shape[1]
     order = far_first(n)
 
@@ -296,10 +297,11 @@
         )
         for item, (source, target) in enumerate(big_pairs)
     ]
-    own.append(pltpu.make_async_copy(big_read.at[read_rows, :], read_big, own_sem.at[3]))
+    own.append(pltpu.make_async_copy(big_read.at[:, read_rows], read_big, own_sem.at[3]))
     own.append(
-        pltpu.make_async_copy(small_read.at[few_read_rows, :], read_small, own_sem.at[4])
-    )
+        pltpu.make_async_copy(small_read.at[:, few_read_rows], read_small, own_sem.at[4])
+    )
+    own.append(pltpu.make_async_copy(guidance, guide, own_sem.at[8]))
     few_own = [
         pltpu.make_async_copy(
             window(source, me, few_width), few_land(target, me, 0), own_sem.at[5 + item]
@@ -332,12 +334,14 @@
 
     for copy in own:
         copy.wait()
-    weight_value = guidance[0]
+    weight_value = guide[0]
     lanes = lax.broadcasted_iota(jnp.int32, (latent.shape[0] // 2, 2 * lat), 1)
 
     def paired(attended, readout):
-        doubled = jnp.concatenate([readout, readout], axis=1)
-        latent[...] = jnp.dot(attended, doubled, preferred_element_type=jnp.float32)
+        doubled = jnp.concatenate([readout, readout], axis=0)
+        latent[...] = lax.dot_general(
+            attended, doubled, (((1,), (1,)), ((), ())), preferred_element_type=jnp.float32
+        )
         even = latent[pl.ds(0, latent.shape[0] // 2, stride=2), :]
         odd = latent[pl.ds(1, latent.shape[0] // 2, stride=2), :]
         return jnp.where(lanes < lat, even, odd)
@@ -434,9 +438,8 @@
     dma = pltpu.SemaphoreType.DMA
     return pl.pallas_call(
         functools.partial(fused_kernel, n, m),
-        out_shape=jax.ShapeDtypeStruct((half, 2 * lat), jnp.float32),
-        in_specs=[pl.BlockSpec(memory_space=pltpu.SMEM)]
-        + [pl.BlockSpec(memory_space=pl.ANY)] * 8,
+        out_shape=pltpu.VMEM((half, 2 * lat), jnp.float32),
+        in_specs=[pl.BlockSpec(memory_space=pl.ANY)] * 9,
         out_specs=pl.BlockSpec(memory_space=pltpu.VMEM),
         scratch_shapes=[
             pltpu.VMEM((tokens, width), kind),
@@ -445,14 +448,15 @@
             pltpu.VMEM((tokens, few_width), kind),
             pltpu.VMEM((tokens, few_width), kind),
             pltpu.VMEM((tokens, few_width), kind),
-            pltpu.VMEM((width, lat), kind),
-            pltpu.VMEM((few_width, lat), kind),
+            pltpu.VMEM((lat, width), kind),
+            pltpu.VMEM((lat, few_width), kind),
             pltpu.VMEM((width // DH, tokens, tokens), kind),
             pltpu.VMEM((tokens, 2 * lat), jnp.float32),
             pltpu.VMEM((tokens // 2, 2 * lat), jnp.float32),
             pltpu.VMEM((n, half, 2 * lat), jnp.float32),
             pltpu.VMEM((n, m, half, 2 * lat), jnp.float32),
-            dma((8,)),
+            pltpu.SMEM((1,), jnp.float32),
+            dma((9,)),
             dma((3, n)),
             dma((3, n)),
             dma((3, n)),
@@ -470,8 +474,8 @@
         small_queries,
         small_keys,
         small_values,
-        big_readout,
-        small_readout,
+        big_readout.T,
+        small_readout.T,
     )
 
 

time: 31.3 us -> 27.3 us (0.87)
  local copies, waits for them, and re-layouts: 4.03 us -> 0.6 us
  Pallas kernels: 26.4 us -> 25.9 us
    unnamed x5 -> x1, local copies, waits for them, and re-layouts: 4.03 us -> 0.6 us
    pallas_call x1, Pallas kernels: 26.4 us -> 25.9 us  [fused(): pl.pallas_call(functools.partial(fused_kernel, n, m), out_shape=pltpu.VME...]
where the time goes in v2:
time: 27.3 us; the launch traced here: 27.2 us
  Pallas kernels  25.9 us (95%)
  between operations  0.66 us (2%)
  local copies, waits for them, and re-layouts  0.6 us (2%)
    pallas_call x1, Pallas kernels, fused(): pl.pallas_call(functools.partial(fused_kernel, n, m), out_shape=pltpu.VME...  25.9 us
    unnamed x1, local copies, waits for them, and re-layouts  0.6 us

profile of v2, /device:TPU:0, one launch (start us, length us, event | category | flops | bytes accessed | tf_op | source)
XLA Modules:
  0.0 27.2 jit_solution(100536839201472979)
XLA Ops:
  0.7 25.9 %fused_window.1 = f32[16,128]{1,0:T(8,128)S(1)} custom-call(f32[1]{0:T(128)S(6)} %copy.12.guidance, bf16[32,2048]{1,0:T(8,128)(2,1)} %big_q.1, bf16[32,2048]{1,0:T(8,128)(2,1)} %big_k.1, bf16[32,2048]{1,0:T(8,128)(2,1)} %big_v.1, bf16[16,1024]{1,0:T(8,128)(2,1)} %small_q.1, bf16[16,1024]{1,0:T(8,128)(2,1)} %small_k.1, bf16[16,1024]{1,0:T(8,128)(2,1)} %small_v.1, ...), custom_call_target="tpu_custom_call" | custom-call | tf_op jit(solution)/shard_map/fused_window/pallas_call | solution.py:439
  26.6 0.6 %copy.11 = f32[16,128]{1,0:T(8,128)} copy(f32[16,128]{1,0:T(8,128)S(1)} %fused_window.1) | data formatting | bytes 16384
